TPU v7x, 256 devices: a whole 4x4x8 slice. The times are simulated.
256 devices in a mesh: expert: 16 (over y, x), tensor: 16 (over z, core).
Axes of the slice: x: 4, y: 4, z: 8, core: 2. Of those that a mesh axis runs over, the one named last changes fastest.
Arguments:
- queries: bfloat16 [4096, 8192], P('expert', 'tensor'), may hold values from -8 to 8
- keys_values: bfloat16 [16, 4, 1280, 256], P('expert'), may hold values from -6 to 6
- prefix_len: int32 [16], P('expert'), may hold values from 128 to 1024, as said below
- out_proj: bfloat16 [8192, 4096], P('tensor', 'expert'), may hold values from -0.0625 to 0.0625
- residual: bfloat16 [4096, 4096], P(('expert', 'tensor')), may hold values from -1.796875 to 1.796875
- norm_gain: float32 [4096], replicated, may hold values from 0.1 to 1.9
- expert_ids: int32 [4096, 8], P('expert'), may hold values from 0 to 63, all different within a row; in each aligned block of 16 rows (0 to 15, 16 to 31, ...) at most 3 rows name the same one
- route_weights: bfloat16 [4096, 8], P('expert'), may hold values from 0.19921875 to 1
- w_gate: bfloat16 [256, 4096, 384], P(('expert', 'tensor')), may hold values from -0.09375 to 0.09375
- w_up: bfloat16 [256, 4096, 384], P(('expert', 'tensor')), may hold values from -0.09375 to 0.09375
- w_down: bfloat16 [256, 384, 4096], P(('expert', 'tensor')), may hold values from -0.15625 to 0.15625
Outputs:
- layer_out: bfloat16 [4096, 4096], P(('expert', 'tensor'))
Inputs may be any that keep to these rules, and one draw needn't show every extreme that they name: `expert_ids`: in the rows of one device (aligned blocks of 16 rows) no expert is named by more than 3 rows, a bound that some block reaches; a row names 8 different experts. `prefix_len`: some sequence has all 1024 slots live.
All inputs are finite; a program needn't handle non-finite values.
Results may differ from a plain program's by a relative error of at most 0.035.
Values may be sent and summed in bfloat16 or wider, within the bound.
No kernel may reach another device: no remote copies, remote signals or barrier semaphores. Data moves between devices by JAX's collectives and lax.ppermute only.
A program may use at most 128 MiB of HBM per device.

v0:
```python
import math
import jax
import jax.numpy as jnp
from jax import lax
from jax.sharding import PartitionSpec as P

HEADS = 64
KVH = 4
HD = 128
TOPK = 8
HSPLIT = 4
TOK_DEV = 16
PREFIX = 1024
MOST = 3
F32 = jnp.float32
BF16 = jnp.bfloat16


def chip_swap(array, tensor_count):
    return lax.ppermute(array, "tensor", [(t, t ^ 1) for t in range(tensor_count)])


def along_z(array, groups):
    return lax.all_to_all(
        array, "tensor", split_axis=0, concat_axis=0, tiled=True, axis_index_groups=groups
    )


def attend(queries, keys_values, prefix_len, kv_index):
    step_rows = queries.shape[0]
    per_device = queries.shape[1] // HD
    cached = lax.dynamic_index_in_dim(keys_values[0], kv_index, 0, keepdims=False)
    key_rows = cached[:, :HD]
    value_rows = cached[:, HD:]
    context = cached.shape[0]
    query_rows = queries.reshape(step_rows, per_device, HD)
    scores = jnp.einsum(
        "nhd,cd->hnc", query_rows, key_rows, preferred_element_type=F32
    ) / math.sqrt(HD)
    columns = jnp.arange(context, dtype=jnp.int32)[None, :]
    positions = jnp.arange(step_rows, dtype=jnp.int32)[:, None]
    visible = ((columns < prefix_len[0]) | (columns >= PREFIX) & (columns - PREFIX <= positions))[
        None
    ]
    highest = jnp.max(jnp.where(visible, scores, -1e30), axis=-1, keepdims=True)
    weights = jnp.exp(jnp.where(visible, scores - highest, -1e30))
    summed = jnp.sum(weights, axis=-1)
    blended = jnp.einsum(
        "hnc,cd->nhd", weights.astype(BF16), value_rows, preferred_element_type=F32
    )
    attended = (blended / jnp.transpose(summed)[:, :, None]).astype(BF16)
    return attended.reshape(step_rows, per_device * HD)


def shards(
    queries,
    keys_values,
    prefix_len,
    out_proj,
    residual,
    norm_gain,
    expert_ids,
    route_weights,
    w_gate,
    w_up,
    w_down,
):
    tensor_count = lax.axis_size("tensor")
    expert_count = lax.axis_size("expert")
    tensor_index = lax.axis_index("tensor")
    chips = tensor_count // 2
    core = tensor_index % 2
    same_core = [[2 * z + c for z in range(chips)] for c in range(2)]
    per_device = queries.shape[1] // HD
    width = residual.shape[1]
    half_rows = chips * TOK_DEV
    gate_other = chip_swap(w_gate[0], tensor_count)
    up_other = chip_swap(w_up[0], tensor_count)
    down_other = chip_swap(w_down[0], tensor_count)
    slot_index = tensor_index // HSPLIT
    slot_count = tensor_count // HSPLIT
    capacity = chips * MOST
    ids = expert_ids.reshape(chips, 2, TOK_DEV, TOPK)
    ids = lax.dynamic_index_in_dim(ids, core, 1, keepdims=False)
    gains = route_weights.reshape(chips, 2, TOK_DEV, TOPK)
    gains = lax.dynamic_index_in_dim(gains, core, 1, keepdims=False)
    wanted = jnp.arange(expert_count, dtype=jnp.int32) * slot_count + slot_index
    named = ids[:, :, :, None] == wanted
    hits = jnp.sum(named.astype(jnp.int32), axis=2)
    weight = jnp.sum(jnp.where(named, gains[:, :, :, None].astype(F32), 0.0), axis=2)
    earlier = (jnp.arange(TOK_DEV)[:, None] > jnp.arange(TOK_DEV)[None, :]).astype(BF16)
    rank = jnp.einsum("nm,zmj->znj", earlier, hits.astype(BF16), preferred_element_type=F32)
    position = jnp.arange(chips, dtype=jnp.int32)[:, None, None] * MOST + rank.astype(jnp.int32)
    position = jnp.where(hits > 0, position, -1).reshape(half_rows, expert_count)
    weight = weight.reshape(half_rows, expert_count)
    slots = jnp.arange(capacity, dtype=jnp.int32)
    pick = (position.T[:, None, :] == slots[None, :, None]).astype(BF16)
    pick = pick.reshape(expert_count * capacity, half_rows)
    combine = jnp.where(position[:, :, None] == slots[None, None, :], weight[:, :, None], 0.0)
    combine = combine.astype(BF16).reshape(half_rows, expert_count * capacity)
    attended = attend(queries, keys_values, prefix_len, tensor_index * per_device // (HEADS // KVH))
    projection = lax.all_gather(out_proj, "expert", axis=1, tiled=True)
    attended = attended.reshape(chips, 2, TOK_DEV, per_device * HD)
    attended_away = lax.dynamic_index_in_dim(attended, 1 - core, 1, keepdims=False)
    attended_here = lax.dynamic_index_in_dim(attended, core, 1, keepdims=False)
    part_away = jnp.dot(
        attended_away.reshape(half_rows, -1), projection, preferred_element_type=F32
    ).astype(BF16)
    part_away = chip_swap(part_away, tensor_count)
    part_here = jnp.dot(
        attended_here.reshape(half_rows, -1), projection, preferred_element_type=F32
    ).astype(BF16)
    chip_part = (part_here.astype(F32) + part_away.astype(F32)).astype(BF16)
    head_parts = along_z(chip_part.reshape(chips, TOK_DEV, width), same_core)
    head_sum = jnp.sum(head_parts.astype(F32), axis=0)
    hidden_state = (residual.astype(F32) + head_sum).astype(BF16)
    values = hidden_state.astype(F32)
    factor = lax.rsqrt(jnp.mean(values * values, axis=-1, keepdims=True) + 1e-06)
    normed = (values * factor * norm_gain[None, :]).astype(BF16)
    normed_half = along_z(jnp.broadcast_to(normed[None], (chips,) + normed.shape), same_core)
    outgoing = jnp.dot(
        pick, normed_half.reshape(half_rows, width), preferred_element_type=F32
    ).astype(BF16)
    arrived = lax.all_to_all(
        outgoing.reshape(expert_count, capacity, width),
        "expert",
        split_axis=0,
        concat_axis=0,
        tiled=True,
    )
    rows = arrived.reshape(expert_count * capacity, width)

    def inner_of(gate, up):
        gate_val = jnp.dot(rows, gate, preferred_element_type=F32)
        up_val = jnp.dot(rows, up, preferred_element_type=F32)
        return (jax.nn.silu(gate_val) * up_val).astype(BF16)

    result = jnp.dot(inner_of(w_gate[0], w_up[0]), w_down[0], preferred_element_type=F32)
    result = result + jnp.dot(
        inner_of(gate_other, up_other), down_other, preferred_element_type=F32
    )
    result = result.astype(BF16).reshape(expert_count, capacity, width)
    returned = lax.all_to_all(result, "expert", split_axis=0, concat_axis=0, tiled=True)
    expert_part = jnp.dot(
        combine, returned.reshape(expert_count * capacity, width), preferred_element_type=F32
    )
    expert_parts = along_z(expert_part.astype(BF16).reshape(chips, TOK_DEV, width), same_core)
    expert_sum = jnp.sum(expert_parts.astype(F32), axis=0)
    return (hidden_state.astype(F32) + expert_sum).astype(BF16)


def solution(mesh):
    return jax.shard_map(
        shards,
        mesh=mesh,
        in_specs=(
            P("expert", "tensor"),
            P("expert", None, None, None),
            P("expert"),
            P("tensor", "expert"),
            P(("expert", "tensor"), None),
            P(),
            P("expert", None),
            P("expert", None),
            P(("expert", "tensor"), None, None),
            P(("expert", "tensor"), None, None),
            P(("expert", "tensor"), None, None),
        ),
        out_specs=P(("expert", "tensor"), None),
        check_vma=False,
    )
```

profile of v0, /device:TPU:24, one launch (start us, length us, event | category | flops | bytes accessed | tf_op | source)
XLA Modules:
  0.0 327.5 jit_solution(82748444382406741)
XLA Ops:
  6.5 0.7 all-gather.2.cloned.1.call-update
  8.0 0.3 copy-done
  8.3 2.0 fusion.13
  10.4 5.1 %fusion.70 = (f32[4,256]{1,0:T(4,128)S(1)}, bf16[4,256,1280]{1,2,0:T(8,128)(2,1)}) fusion(pred[256,1280]{0,1:T(8,128)(4,1)} %fusion.13, bf16[1280,256]{1,0:T(8,128)(2,1)S(1)} %dynamic-slice_bitcast_fusion, bf16[256,512]{1,0:T(8,128)(2,1)} %param.11), kind=kOutput, calls=%fused_computation.92 | convolution fusion | flops 680264960 | bytes 4460544 | tf_op jit(solution)/shard_map/sub | solution.py:46
  15.5 2.3 fusion.21
  17.7 0.2 copy.34
  17.9 0.1 reshape_reshape.3
  18.1 56.6 %all-gather.2.cloned.1.call-done = bf16[512,4096]{1,0:T(8,128)(2,1)} async-done(((bf16[512,256]{1,0:T(8,128)(2,1)}), bf16[512,4096]{1,0:T(8,128)(2,1)}) %all-gather.2.cloned.1.call-update) | async-done | bytes 4194320 | tf_op jit(solution)/shard_map/all_gather | solution.py:102
  74.7 3.1 convolution_convert_fusion.1
  77.8 0.1 collective-permute-start
  77.9 2.6 collective-permute-done
  80.5 0.7 add_convert_fusion.1
  81.2 0.0 copy-start.2
  81.3 0.0 copy-start.3
  81.3 36.0 %all_to_all.25 = bf16[8,16,4096]{2,1,0:T(8,128)(2,1)S(1)} all-to-all(bf16[8,16,4096]{2,1,0:T(8,128)(2,1)S(1)} %bitcast.116), channel_id=1, replica_groups={{0,2,4,6,8,10,12,14},{1,3,5,7,9,11,13,15},{16,18,20,22,24,26,28,30},{17..., dimensions={0} | all-to-all | bytes 2097152 | tf_op jit(solution)/shard_map/all_to_all | solution.py:24
  117.2 0.1 convert_reduce_fusion.1
  117.4 0.2 fusion.39
  117.6 0.1 fusion.41
  117.7 1.1 broadcast_in_dim.76
  118.8 4.2 %all-to-all-start.1 = ((bf16[8,16,4096]{2,1,0:T(8,128)(2,1)}), bf16[8,16,4096]{2,1,0:T(8,128)(2,1)}, u32[]{:S(2)}, u32[]{:S(2)}) async-start(bf16[8,16,4096]{2,1,0:T(8,128)(2,1)} %broadcast_in_dim.76), calls=%async_computation.1 | async-start | bytes 2097152 | tf_op jit(solution)/shard_map/all_to_all | solution.py:24
  123.0 0.1 reshape.179
  123.2 0.1 copy.36
  123.3 0.2 fusion.35
  123.6 0.1 copy.37
  123.6 0.2 fusion.27
  123.9 0.1 eq.59
  124.0 26.9 %all-to-all-done.1 = bf16[8,16,4096]{2,1,0:T(8,128)(2,1)} async-done(((bf16[8,16,4096]{2,1,0:T(8,128)(2,1)}), bf16[8,16,4096]{2,1,0:T(8,128)(2,1)}, u32[]{:S(2)}, u32[]{:S(2)}) %all-to-all-start.1) | async-done | bytes 1048608 | tf_op jit(solution)/shard_map/all_to_all | solution.py:24
  150.9 3.8 %convolution_convert_fusion = bf16[384,4096]{1,0:T(8,128)(2,1)} fusion(pred[384,128]{1,0:T(8,128)(4,1)S(1)} %bitcast.122, bf16[128,4096]{1,0:T(8,128)(2,1)} %bitcast.17), kind=kOutput, calls=%fused_computation.2 | convolution fusion | flops 404226048 | bytes 4243456 | tf_op jit(solution)/shard_map/dot_general | solution.py:121
  154.8 5.7 %all-to-all-start.2 = ((bf16[16,24,4096]{2,1,0:T(8,128)(2,1)}), bf16[16,24,4096]{2,1,0:T(8,128)(2,1)}, u32[]{:S(2)}, u32[]{:S(2)}) async-start(bf16[16,24,4096]{2,1,0:T(8,128)(2,1)} %bitcast.114), calls=%async_computation.2 | async-start | bytes 6291456 | tf_op jit(solution)/shard_map/all_to_all | solution.py:124
  160.5 0.0 collective-permute-start.1
  160.5 0.5 collective-permute-start.3
  161.0 0.1 collective-permute-start.2
  161.1 46.1 %all-to-all-done.2 = bf16[16,24,4096]{2,1,0:T(8,128)(2,1)} async-done(((bf16[16,24,4096]{2,1,0:T(8,128)(2,1)}), bf16[16,24,4096]{2,1,0:T(8,128)(2,1)}, u32[]{:S(2)}, u32[]{:S(2)}) %all-to-all-start.2) | async-done | bytes 3145760 | tf_op jit(solution)/shard_map/all_to_all | solution.py:124
  207.2 5.4 %fusion.63 = f32[384,384]{1,0:T(8,128)} fusion(bf16[384,4096]{1,0:T(8,128)(2,1)} %bitcast.19, bf16[1,4096,384]{2,1,0:T(8,128)(2,1)} %param.19), kind=kOutput, calls=%fused_computation.85 | convolution fusion | flops 1207959552 | bytes 6881280 | tf_op jit(solution)/shard_map/dot_general | solution.py:134
  212.7 0.0 collective-permute-done.1
  212.7 4.6 %fusion.77 = f32[384,384]{1,0:T(8,128)S(1)} fusion(bf16[384,4096]{1,0:T(8,128)(2,1)} %bitcast.19, bf16[4096,384]{1,0:T(8,128)(2,1)} %collective-permute-done.1), kind=kOutput, calls=%fused_computation.94 | convolution fusion | flops 1207959552 | bytes 6881280 | tf_op jit(solution)/shard_map/dot_general | solution.py:134
  217.3 10.0 %fusion.24 = f32[384,4096]{1,0:T(8,128)} fusion(bf16[384,4096]{1,0:T(8,128)(2,1)} %bitcast.19, f32[384,384]{1,0:T(8,128)} %fusion.63, bf16[1,384,4096]{2,1,0:T(8,128)(2,1)} %param.21, bf16[1,4096,384]{2,1,0:T(8,128)(2,1)} %param.20), kind=kOutput, calls=%fused_computation.30 | convolution fusion | flops 2416803840 | bytes 16318464 | tf_op jit(solution)/shard_map/dot_general | solution.py:138
  227.4 10.7 %add_convert_fusion = bf16[384,4096]{1,0:T(8,128)(2,1)} fusion(f32[384,4096]{1,0:T(8,128)} %fusion.24, bf16[384,4096]{1,0:T(8,128)(2,1)} %collective-permute-done.3, f32[384,384]{1,0:T(8,128)S(1)} %fusion.77, bf16[384,4096]{1,0:T(8,128)(2,1)} %bitcast.19, bf16[4096,384]{1,0:T(8,128)(2,1)} %collective-permute-done.2), kind=kOutput, calls=%fused_computation.1 | convolution fusion | flops 2419949568 | bytes 19464192 | tf_op jit(solution)/shard_map/dot_general | solution.py:139
  238.0 6.0 %all-to-all-start.3 = ((bf16[16,24,4096]{2,1,0:T(8,128)(2,1)}), bf16[16,24,4096]{2,1,0:T(8,128)(2,1)}, u32[]{:S(2)}, u32[]{:S(2)}) async-start(bf16[16,24,4096]{2,1,0:T(8,128)(2,1)} %bitcast.115), calls=%async_computation.3 | async-start | bytes 6291456 | tf_op jit(solution)/shard_map/all_to_all | solution.py:143
  244.0 0.1 reshape.180
  244.2 0.1 copy.40
  244.3 0.4 fusion.36
  244.6 0.1 copy.41
  244.7 43.3 %all-to-all-done.3 = bf16[16,24,4096]{2,1,0:T(8,128)(2,1)} async-done(((bf16[16,24,4096]{2,1,0:T(8,128)(2,1)}), bf16[16,24,4096]{2,1,0:T(8,128)(2,1)}, u32[]{:S(2)}, u32[]{:S(2)}) %all-to-all-start.3) | async-done | bytes 3145760 | tf_op jit(solution)/shard_map/all_to_all | solution.py:143
  288.0 2.6 fusion.5
  290.6 29.2 %all_to_all.26 = bf16[8,16,4096]{2,1,0:T(8,128)(2,1)S(1)} all-to-all(bf16[8,16,4096]{2,1,0:T(8,128)(2,1)S(1)} %bitcast.117), channel_id=1, replica_groups={{0,2,4,6,8,10,12,14},{1,3,5,7,9,11,13,15},{16,18,20,22,24,26,28,30},{17..., dimensions={0} | all-to-all | bytes 2097152 | tf_op jit(solution)/shard_map/all_to_all | solution.py:24
  319.8 0.1 convert_reduce_fusion
  320.0 0.7 fusion.42
  (23 shorter events, 0.2 us)
Async XLA Ops:
  6.5 1.7 copy-start
  6.5 68.2 %all-gather.2.cloned.1.call-start = ((), (), s32[]{:S(2)}) async-start(), calls=%async_computation.5 | async-start | bytes 4456448 | tf_op jit(solution)/shard_map/all_gather | solution.py:102
  74.7 5.8 %copy-start.1 = (bf16[512,4096]{1,0:T(8,128)(2,1)S(1)}, bf16[512,4096]{1,0:T(8,128)(2,1)}, u32[]{:S(2)}) copy-start(bf16[512,4096]{1,0:T(8,128)(2,1)} %all-gather.2.cloned.1.call-done) | copy-start | bytes 12582916
  77.8 2.7 collective-permute-start
  81.2 36.1 %copy-start.2 = (bf16[16,4096]{1,0:T(8,128)(2,1)S(1)}, bf16[16,4096]{1,0:T(8,128)(2,1)}, u32[]{:S(2)}) copy-start(bf16[16,4096]{1,0:T(8,128)(2,1)} %param.15) | copy-start | bytes 393220
  81.3 36.3 %copy-start.3 = (f32[4096]{0:T(1024)S(1)}, f32[4096]{0:T(1024)}, u32[]{:S(2)}) copy-start(f32[4096]{0:T(1024)} %param.16) | copy-start | bytes 49156
  117.2 5.8 %copy-start.4 = (s32[256,8]{0,1:T(8,128)S(1)}, s32[256,8]{0,1:T(8,128)}, u32[]{:S(2)}) copy-start(s32[256,8]{0,1:T(8,128)} %param.17) | copy-start | bytes 24580
  118.8 32.2 %all-to-all-start.1 = ((bf16[8,16,4096]{2,1,0:T(8,128)(2,1)}), bf16[8,16,4096]{2,1,0:T(8,128)(2,1)}, u32[]{:S(2)}, u32[]{:S(2)}) async-start(bf16[8,16,4096]{2,1,0:T(8,128)(2,1)} %broadcast_in_dim.76), calls=%async_computation.1 | async-start | bytes 2097152 | tf_op jit(solution)/shard_map/all_to_all | solution.py:24
  154.8 52.5 %all-to-all-start.2 = ((bf16[16,24,4096]{2,1,0:T(8,128)(2,1)}), bf16[16,24,4096]{2,1,0:T(8,128)(2,1)}, u32[]{:S(2)}, u32[]{:S(2)}) async-start(bf16[16,24,4096]{2,1,0:T(8,128)(2,1)} %bitcast.114), calls=%async_computation.2 | async-start | bytes 6291456 | tf_op jit(solution)/shard_map/all_to_all | solution.py:124
  160.5 52.2 %collective-permute-start.1 = (bf16[4096,384]{1,0:T(8,128)(2,1)}, bf16[4096,384]{1,0:T(8,128)(2,1)}, u32[]{:S(2)}, u32[]{:S(2)}) collective-permute-start(bf16[4096,384]{1,0:T(8,128)(2,1)} %bitcast.127), channel_id=1, source_target_pairs={{0,1},{1,0},{2,3},{3,2},{4,5},{5,4},{6,7},{7,6},{8,9},{9,8},{10,11... | collective-permute-start | bytes 9437192 | tf_op jit(solution)/shard_map/ppermute | solution.py:20
  160.5 66.8 %collective-permute-start.3 = (bf16[384,4096]{1,0:T(8,128)(2,1)}, bf16[384,4096]{1,0:T(8,128)(2,1)}, u32[]{:S(2)}, u32[]{:S(2)}) collective-permute-start(bf16[384,4096]{1,0:T(8,128)(2,1)} %bitcast.118), channel_id=1, source_target_pairs={{0,1},{1,0},{2,3},{3,2},{4,5},{5,4},{6,7},{7,6},{8,9},{9,8},{10,11... | collective-permute-start | bytes 9437192 | tf_op jit(solution)/shard_map/ppermute | solution.py:20
  161.0 66.4 %collective-permute-start.2 = (bf16[4096,384]{1,0:T(8,128)(2,1)}, bf16[4096,384]{1,0:T(8,128)(2,1)}, u32[]{:S(2)}, u32[]{:S(2)}) collective-permute-start(bf16[4096,384]{1,0:T(8,128)(2,1)} %bitcast.119), channel_id=1, source_target_pairs={{0,1},{1,0},{2,3},{3,2},{4,5},{5,4},{6,7},{7,6},{8,9},{9,8},{10,11... | collective-permute-start | bytes 9437192 | tf_op jit(solution)/shard_map/ppermute | solution.py:20
  238.0 6.0 %copy-start.5 = (bf16[256,8]{0,1:T(8,128)(2,1)S(1)}, bf16[256,8]{0,1:T(8,128)(2,1)}, u32[]{:S(2)}) copy-start(bf16[256,8]{0,1:T(8,128)(2,1)} %param.18) | copy-start | bytes 12292
  238.0 50.0 %all-to-all-start.3 = ((bf16[16,24,4096]{2,1,0:T(8,128)(2,1)}), bf16[16,24,4096]{2,1,0:T(8,128)(2,1)}, u32[]{:S(2)}, u32[]{:S(2)}) async-start(bf16[16,24,4096]{2,1,0:T(8,128)(2,1)} %bitcast.115), calls=%async_computation.3 | async-start | bytes 6291456 | tf_op jit(solution)/shard_map/all_to_all | solution.py:143
Sparse Core Ops, SparseCore 0:
  9.8 64.8 all-gather.1
where the time goes:
time: 328 us; the launch traced here: 327 us
  waiting for transfers between devices  176 us (54%)
  blocking collectives  65.2 us (20%)
  matrix products  48.6 us (15%)
  starting transfers between devices  16.7 us (5%)
  between operations  14.4 us (4%)
  other arithmetic  3.96 us (1%)
    all_to_all x2, blocking collectives, along_z(): lax.all_to_all(array, 'tensor', split_axis=0, concat_axis=0, tiled=True,...  65.2 us
    all_gather x1, waiting for transfers between devices, shards(): projection = lax.all_gather(out_proj, 'expert', axis=1, tiled=True)  56.6 us
    all_to_all x1, waiting for transfers between devices, shards(): lax.all_to_all(outgoing.reshape(expert_count, capacity, width), 'expert',...  46.1 us
    all_to_all x1, waiting for transfers between devices, shards(): lax.all_to_all(result, 'expert', split_axis=0, concat_axis=0, tiled=True)  43.3 us
    all_to_all x1, waiting for transfers between devices, along_z(): lax.all_to_all(array, 'tensor', split_axis=0, concat_axis=0, tiled=True,...  26.9 us
    dot_general x1, matrix products, shards(): jnp.dot(inner_of(gate_other, up_other), down_other, preferred_element_typ...  10.7 us
    dot_general x2, matrix products, inner_of(): gate_val = jnp.dot(rows, gate, preferred_element_type=F32)  10.1 us
    dot_general x1, matrix products, shards(): jnp.dot(inner_of(w_gate[0], w_up[0]), w_down[0], preferred_element_type=F32)  10 us
  transfers between devices with their start and end apart: 8, of which 5 were waited for; matrix products, arithmetic and copies ran while one was open for 10% of the time, Pallas kernels for 0%

commit v1 on v0

--- a/solution.py
+++ b/solution.py
@@ -99,7 +99,8 @@
     combine = jnp.where(position[:, :, None] == slots[None, None, :], weight[:, :, None], 0.0)
     combine = combine.astype(BF16).reshape(half_rows, expert_count * capacity)
     attended = attend(queries, keys_values, prefix_len, tensor_index * per_device // (HEADS // KVH))
-    projection = lax.all_gather(out_proj, "expert", axis=1, tiled=True)
+    copies = jnp.concatenate([out_proj] * lax.axis_size("expert"), axis=1)
+    projection = lax.all_to_all(copies, "expert", 1, 1, tiled=True)
     attended = attended.reshape(chips, 2, TOK_DEV, per_device * HD)
     attended_away = lax.dynamic_index_in_dim(attended, 1 - core, 1, keepdims=False)
     attended_here = lax.dynamic_index_in_dim(attended, core, 1, keepdims=False)

time: 328 us -> 334 us (1.018)
  local copies, waits for them, and re-layouts: 2.39 us -> 18.5 us
  between operations: 14.4 us -> 1.11 us
  starting transfers between devices: 16.7 us -> 23.4 us
    all_gather x1 -> x0, waiting for transfers between devices: 56.6 us -> none  [shards(): projection = lax.all_gather(out_proj, 'expert', axis=1, tiled=True)]
    all_to_all x0 -> x1, waiting for transfers between devices: none -> 53.7 us  [shards(): projection = lax.all_to_all(copies, 'expert', 1, 1, tiled=True)]
    all_to_all x0 -> x2, local copies, waits for them, and re-layouts: none -> 12.9 us  [shards(): projection = lax.all_to_all(copies, 'expert', 1, 1, tiled=True)]
    all_to_all x0 -> x1, starting transfers between devices: none -> 7.3 us  [shards(): projection = lax.all_to_all(copies, 'expert', 1, 1, tiled=True)]
  transfers between devices with their start and end apart: 8 -> 8, of which waited for: 5 -> 5; matrix products, arithmetic and copies ran while one was open for 10% -> 8% of each run, Pallas kernels for 0% -> 0%
where the time goes in v1:
time: 334 us; the launch traced here: 333 us
  waiting for transfers between devices  173 us (52%)
  blocking collectives  66.9 us (20%)
  matrix products  46.6 us (14%)
  starting transfers between devices  23.4 us (7%)
  local copies, waits for them, and re-layouts  18.5 us (6%)
    all_to_all x2, blocking collectives, along_z(): lax.all_to_all(array, 'tensor', split_axis=0, concat_axis=0, tiled=True,...  66.9 us
    all_to_all x1, waiting for transfers between devices, shards(): projection = lax.all_to_all(copies, 'expert', 1, 1, tiled=True)  53.7 us
    all_to_all x1, waiting for transfers between devices, shards(): lax.all_to_all(outgoing.reshape(expert_count, capacity, width), 'expert',...  46.3 us
    all_to_all x1, waiting for transfers between devices, shards(): lax.all_to_all(result, 'expert', split_axis=0, concat_axis=0, tiled=True)  43.8 us
    all_to_all x1, waiting for transfers between devices, along_z(): lax.all_to_all(array, 'tensor', split_axis=0, concat_axis=0, tiled=True,...  26.8 us
    all_to_all x2, local copies, waits for them, and re-layouts, shards(): projection = lax.all_to_all(copies, 'expert', 1, 1, tiled=True)  12.9 us
    dot_general x1, matrix products, shards(): jnp.dot(inner_of(gate_other, up_other), down_other, preferred_element_typ...  10.7 us
    dot_general x1, matrix products, shards(): jnp.dot(inner_of(w_gate[0], w_up[0]), w_down[0], preferred_element_type=F32)  9.87 us
  transfers between devices with their start and end apart: 8, of which 5 were waited for; matrix products, arithmetic and copies ran while one was open for 8% of the time, Pallas kernels for 0%

profile of v1, /device:TPU:24, one launch (start us, length us, event | category | flops | bytes accessed | tf_op | source)
XLA Modules:
  0.0 332.8 jit_solution(3476188151573780845)
XLA Ops:
  0.0 1.2 copy.69
  1.7 1.9 copy-done.3
  3.6 6.4 %copy.85 = bf16[512,16,256]{2,0,1:T(8,128)(2,1)} copy(bf16[512,16,256]{0,2,1:T(8,128)(2,1)} %bitcast.120) | data formatting | bytes 8388608 | tf_op jit(solution)/shard_map/all_to_all | solution.py:103
  10.1 7.3 %all-to-all-start = ((bf16[512,16,256]{2,0,1:T(8,128)(2,1)}), bf16[512,16,256]{2,0,1:T(8,128)(2,1)}, u32[]{:S(2)}, u32[]{:S(2)}) async-start(bf16[512,16,256]{2,0,1:T(8,128)(2,1)} %copy.85), calls=%async_computation | async-start | bytes 8388608 | tf_op jit(solution)/shard_map/all_to_all | solution.py:103
  18.0 0.1 dynamic-slice_bitcast_fusion
  18.1 1.0 fusion.13
  19.2 3.9 %fusion.70 = (f32[4,256]{1,0:T(4,128)S(1)}, bf16[4,256,1280]{1,2,0:T(8,128)(2,1)}) fusion(pred[256,1280]{0,1:T(8,128)(4,1)S(1)} %fusion.13, bf16[1280,256]{1,0:T(8,128)(2,1)S(1)} %dynamic-slice_bitcast_fusion, bf16[256,512]{1,0:T(8,128)(2,1)S(1)} %copy-done.8), kind=kOutput, calls=%fused_computation.108 | convolution fusion | flops 680264960 | bytes 4460544 | tf_op jit(solution)/shard_map/sub | solution.py:46
  23.0 2.3 fusion.21
  25.3 0.2 copy.68
  25.5 0.1 reshape_reshape.3
  25.6 53.7 %all-to-all-done = bf16[512,16,256]{2,0,1:T(8,128)(2,1)} async-done(((bf16[512,16,256]{2,0,1:T(8,128)(2,1)}), bf16[512,16,256]{2,0,1:T(8,128)(2,1)}, u32[]{:S(2)}, u32[]{:S(2)}) %all-to-all-start) | async-done | bytes 4194336 | tf_op jit(solution)/shard_map/all_to_all | solution.py:103
  79.4 6.4 %copy.86 = bf16[512,16,256]{0,2,1:T(8,128)(2,1)} copy(bf16[512,16,256]{2,0,1:T(8,128)(2,1)} %all-to-all-done) | data formatting | bytes 8388608 | tf_op jit(solution)/shard_map/all_to_all | solution.py:103
  85.8 3.8 %convolution_convert_fusion.1 = bf16[128,4096]{1,0:T(8,128)(2,1)S(1)} fusion(bf16[128,512]{1,0:T(8,128)(2,1)S(1)} %bitcast.127, bf16[512,4096]{0,1:T(8,128)(2,1)} %bitcast.116), kind=kOutput, calls=%fused_computation.11 | convolution fusion | flops 537395200 | bytes 5373952 | tf_op jit(solution)/shard_map/dot_general | solution.py:107
  89.6 0.1 collective-permute-start
  89.7 2.6 collective-permute-done
  92.4 1.5 add_convert_fusion.1
  93.9 37.3 %all_to_all.37 = bf16[8,16,4096]{2,1,0:T(8,128)(2,1)S(1)} all-to-all(bf16[8,16,4096]{2,1,0:T(8,128)(2,1)S(1)} %bitcast.121), channel_id=1, replica_groups={{0,2,4,6,8,10,12,14},{1,3,5,7,9,11,13,15},{16,18,20,22,24,26,28,30},{17..., dimensions={0} | all-to-all | bytes 2097152 | tf_op jit(solution)/shard_map/all_to_all | solution.py:24
  131.2 0.1 convert_reduce_fusion.1
  131.3 0.2 fusion.39
  131.5 0.1 fusion.41
  131.6 1.1 broadcast_in_dim.76
  132.7 3.6 %all-to-all-start.2 = ((bf16[8,16,4096]{2,1,0:T(8,128)(2,1)}), bf16[8,16,4096]{2,1,0:T(8,128)(2,1)S(1)}, u32[]{:S(2)}, u32[]{:S(2)}) async-start(bf16[8,16,4096]{2,1,0:T(8,128)(2,1)} %broadcast_in_dim.76), calls=%async_computation.2 | async-start | bytes 2097152 | tf_op jit(solution)/shard_map/all_to_all | solution.py:24
  136.3 0.1 reshape.181
  136.5 0.1 copy.88
  136.6 0.2 fusion.35
  136.8 0.1 copy.89
  136.9 0.2 fusion.27
  137.1 0.1 eq.59
  137.2 26.8 %all-to-all-done.2 = bf16[8,16,4096]{2,1,0:T(8,128)(2,1)S(1)} async-done(((bf16[8,16,4096]{2,1,0:T(8,128)(2,1)}), bf16[8,16,4096]{2,1,0:T(8,128)(2,1)S(1)}, u32[]{:S(2)}, u32[]{:S(2)}) %all-to-all-start.2) | async-done | bytes 1048608 | tf_op jit(solution)/shard_map/all_to_all | solution.py:24
  164.1 2.6 convolution_convert_fusion
  166.7 5.9 %all-to-all-start.3 = ((bf16[16,24,4096]{2,1,0:T(8,128)(2,1)}), bf16[16,24,4096]{2,1,0:T(8,128)(2,1)}, u32[]{:S(2)}, u32[]{:S(2)}) async-start(bf16[16,24,4096]{2,1,0:T(8,128)(2,1)} %bitcast.118), calls=%async_computation.3 | async-start | bytes 6291456 | tf_op jit(solution)/shard_map/all_to_all | solution.py:125
  172.6 0.5 collective-permute-start.3
  173.1 0.1 collective-permute-start.2
  173.2 46.3 %all-to-all-done.3 = bf16[16,24,4096]{2,1,0:T(8,128)(2,1)} async-done(((bf16[16,24,4096]{2,1,0:T(8,128)(2,1)}), bf16[16,24,4096]{2,1,0:T(8,128)(2,1)}, u32[]{:S(2)}, u32[]{:S(2)}) %all-to-all-start.3) | async-done | bytes 3145760 | tf_op jit(solution)/shard_map/all_to_all | solution.py:125
  219.5 4.6 %fusion.63 = f32[384,384]{1,0:T(8,128)S(1)} fusion(bf16[384,4096]{1,0:T(8,128)(2,1)} %bitcast.21, bf16[1,4096,384]{2,1,0:T(8,128)(2,1)} %param.19), kind=kOutput, calls=%fused_computation.101 | convolution fusion | flops 1207959552 | bytes 6881280 | tf_op jit(solution)/shard_map/dot_general | solution.py:135
  224.1 4.6 %fusion.77 = f32[384,384]{1,0:T(8,128)S(1)} fusion(bf16[384,4096]{1,0:T(8,128)(2,1)} %bitcast.21, bf16[4096,384]{1,0:T(8,128)(2,1)} %collective-permute-done.1), kind=kOutput, calls=%fused_computation.110 | convolution fusion | flops 1207959552 | bytes 6881280 | tf_op jit(solution)/shard_map/dot_general | solution.py:135
  228.7 9.9 %fusion.24 = f32[384,4096]{1,0:T(8,128)} fusion(bf16[384,4096]{1,0:T(8,128)(2,1)} %bitcast.21, f32[384,384]{1,0:T(8,128)S(1)} %fusion.63, bf16[1,384,4096]{2,1,0:T(8,128)(2,1)} %param.21, bf16[1,4096,384]{2,1,0:T(8,128)(2,1)} %param.20), kind=kOutput, calls=%fused_computation.30 | convolution fusion | flops 2416803840 | bytes 16318464 | tf_op jit(solution)/shard_map/dot_general | solution.py:139
  238.6 10.7 %add_convert_fusion = bf16[384,4096]{1,0:T(8,128)(2,1)} fusion(f32[384,4096]{1,0:T(8,128)} %fusion.24, bf16[384,4096]{1,0:T(8,128)(2,1)} %collective-permute-done.3, f32[384,384]{1,0:T(8,128)S(1)} %fusion.77, bf16[384,4096]{1,0:T(8,128)(2,1)} %bitcast.21, bf16[4096,384]{1,0:T(8,128)(2,1)} %collective-permute-done.2), kind=kOutput, calls=%fused_computation.1 | convolution fusion | flops 2419949568 | bytes 19464192 | tf_op jit(solution)/shard_map/dot_general | solution.py:140
  249.3 6.0 %all-to-all-start.4 = ((bf16[16,24,4096]{2,1,0:T(8,128)(2,1)}), bf16[16,24,4096]{2,1,0:T(8,128)(2,1)}, u32[]{:S(2)}, u32[]{:S(2)}) async-start(bf16[16,24,4096]{2,1,0:T(8,128)(2,1)} %bitcast.119), calls=%async_computation.4 | async-start | bytes 6291456 | tf_op jit(solution)/shard_map/all_to_all | solution.py:144
  255.2 0.1 reshape.182
  255.4 0.1 copy.92
  255.4 0.4 fusion.36
  255.8 0.1 copy.93
  255.9 43.8 %all-to-all-done.4 = bf16[16,24,4096]{2,1,0:T(8,128)(2,1)} async-done(((bf16[16,24,4096]{2,1,0:T(8,128)(2,1)}), bf16[16,24,4096]{2,1,0:T(8,128)(2,1)}, u32[]{:S(2)}, u32[]{:S(2)}) %all-to-all-start.4) | async-done | bytes 3145760 | tf_op jit(solution)/shard_map/all_to_all | solution.py:144
  299.7 2.6 fusion.5
  302.3 29.6 %all_to_all.38 = bf16[8,16,4096]{2,1,0:T(8,128)(2,1)S(1)} all-to-all(bf16[8,16,4096]{2,1,0:T(8,128)(2,1)S(1)} %bitcast.122), channel_id=1, replica_groups={{0,2,4,6,8,10,12,14},{1,3,5,7,9,11,13,15},{16,18,20,22,24,26,28,30},{17..., dimensions={0} | all-to-all | bytes 2097152 | tf_op jit(solution)/shard_map/all_to_all | solution.py:24
  331.9 0.1 convert_reduce_fusion
  332.1 0.7 fusion.42
  (47 shorter events, 0.5 us)
Async XLA Ops:
  0.0 18.0 %copy-start = (bf16[1,4,1280,256]{3,2,1,0:T(8,128)(2,1)S(1)}, bf16[1,4,1280,256]{3,2,1,0:T(8,128)(2,1)}, u32[]{:S(2)}) copy-start(bf16[1,4,1280,256]{3,2,1,0:T(8,128)(2,1)} %param.12) | copy-start | bytes 7864324
  1.7 1.9 copy-start.3
  10.0 9.1 %copy-start.8 = (bf16[256,512]{1,0:T(8,128)(2,1)S(1)}, bf16[256,512]{1,0:T(8,128)(2,1)}, u32[]{:S(2)}) copy-start(bf16[256,512]{1,0:T(8,128)(2,1)} %param.11) | copy-start | bytes 786436
  10.1 69.3 %all-to-all-start = ((bf16[512,16,256]{2,0,1:T(8,128)(2,1)}), bf16[512,16,256]{2,0,1:T(8,128)(2,1)}, u32[]{:S(2)}, u32[]{:S(2)}) async-start(bf16[512,16,256]{2,0,1:T(8,128)(2,1)} %copy.85), calls=%async_computation | async-start | bytes 8388608 | tf_op jit(solution)/shard_map/all_to_all | solution.py:103
  85.8 6.6 %copy-start.2 = (bf16[512,16,256]{0,2,1:T(8,128)(2,1)S(1)}, bf16[512,16,256]{0,2,1:T(8,128)(2,1)}, u32[]{:S(2)}) copy-start(bf16[512,16,256]{0,2,1:T(8,128)(2,1)} %copy.86) | copy-start | bytes 12582916
  89.6 2.7 collective-permute-start
  92.4 39.0 %copy-start.4 = (bf16[16,4096]{1,0:T(8,128)(2,1)S(1)}, bf16[16,4096]{1,0:T(8,128)(2,1)}, u32[]{:S(2)}) copy-start(bf16[16,4096]{1,0:T(8,128)(2,1)} %param.15) | copy-start | bytes 393220
  92.4 39.1 %copy-start.5 = (f32[4096]{0:T(1024)S(1)}, f32[4096]{0:T(1024)}, u32[]{:S(2)}) copy-start(f32[4096]{0:T(1024)} %param.16) | copy-start | bytes 49156
  93.9 42.4 %copy-start.6 = (s32[256,8]{0,1:T(8,128)S(1)}, s32[256,8]{0,1:T(8,128)}, u32[]{:S(2)}) copy-start(s32[256,8]{0,1:T(8,128)} %param.17) | copy-start | bytes 24580
  132.7 31.4 %all-to-all-start.2 = ((bf16[8,16,4096]{2,1,0:T(8,128)(2,1)}), bf16[8,16,4096]{2,1,0:T(8,128)(2,1)S(1)}, u32[]{:S(2)}, u32[]{:S(2)}) async-start(bf16[8,16,4096]{2,1,0:T(8,128)(2,1)} %broadcast_in_dim.76), calls=%async_computation.2 | async-start | bytes 2097152 | tf_op jit(solution)/shard_map/all_to_all | solution.py:24
  166.7 52.8 %all-to-all-start.3 = ((bf16[16,24,4096]{2,1,0:T(8,128)(2,1)}), bf16[16,24,4096]{2,1,0:T(8,128)(2,1)}, u32[]{:S(2)}, u32[]{:S(2)}) async-start(bf16[16,24,4096]{2,1,0:T(8,128)(2,1)} %bitcast.118), calls=%async_computation.3 | async-start | bytes 6291456 | tf_op jit(solution)/shard_map/all_to_all | solution.py:125
  172.6 51.5 %collective-permute-start.1 = (bf16[4096,384]{1,0:T(8,128)(2,1)}, bf16[4096,384]{1,0:T(8,128)(2,1)}, u32[]{:S(2)}, u32[]{:S(2)}) collective-permute-start(bf16[4096,384]{1,0:T(8,128)(2,1)} %bitcast.133), channel_id=1, source_target_pairs={{0,1},{1,0},{2,3},{3,2},{4,5},{5,4},{6,7},{7,6},{8,9},{9,8},{10,11... | collective-permute-start | bytes 9437192 | tf_op jit(solution)/shard_map/ppermute | solution.py:20
  172.6 66.0 %collective-permute-start.3 = (bf16[384,4096]{1,0:T(8,128)(2,1)}, bf16[384,4096]{1,0:T(8,128)(2,1)}, u32[]{:S(2)}, u32[]{:S(2)}) collective-permute-start(bf16[384,4096]{1,0:T(8,128)(2,1)} %bitcast.124), channel_id=1, source_target_pairs={{0,1},{1,0},{2,3},{3,2},{4,5},{5,4},{6,7},{7,6},{8,9},{9,8},{10,11... | collective-permute-start | bytes 9437192 | tf_op jit(solution)/shard_map/ppermute | solution.py:20
  173.1 65.5 %collective-permute-start.2 = (bf16[4096,384]{1,0:T(8,128)(2,1)}, bf16[4096,384]{1,0:T(8,128)(2,1)}, u32[]{:S(2)}, u32[]{:S(2)}) collective-permute-start(bf16[4096,384]{1,0:T(8,128)(2,1)} %bitcast.125), channel_id=1, source_target_pairs={{0,1},{1,0},{2,3},{3,2},{4,5},{5,4},{6,7},{7,6},{8,9},{9,8},{10,11... | collective-permute-start | bytes 9437192 | tf_op jit(solution)/shard_map/ppermute | solution.py:20
  249.3 6.0 %copy-start.7 = (bf16[256,8]{0,1:T(8,128)(2,1)S(1)}, bf16[256,8]{0,1:T(8,128)(2,1)}, u32[]{:S(2)}) copy-start(bf16[256,8]{0,1:T(8,128)(2,1)} %param.18) | copy-start | bytes 12292
  249.3 50.4 %all-to-all-start.4 = ((bf16[16,24,4096]{2,1,0:T(8,128)(2,1)}), bf16[16,24,4096]{2,1,0:T(8,128)(2,1)}, u32[]{:S(2)}, u32[]{:S(2)}) async-start(bf16[16,24,4096]{2,1,0:T(8,128)(2,1)} %bitcast.119), calls=%async_computation.4 | async-start | bytes 6291456 | tf_op jit(solution)/shard_map/all_to_all | solution.py:144
  255.4 77.4 %copy-start.1 = (bf16[1,4,1280,256]{3,2,1,0:T(8,128)(2,1)S(1)}, bf16[1,4,1280,256]{3,2,1,0:T(8,128)(2,1)}, u32[]{:S(2)}) copy-start(bf16[1,4,1280,256]{3,2,1,0:T(8,128)(2,1)} %param.12) | copy-start | bytes 7864324
